TPU v7x, 512 devices: a whole 4x4x16 slice. The times are simulated.
512 devices in a mesh: mom: 8 (over y, x_lo), shard: 64 (over x_hi, z, core).
Axes of the slice: x: 4 (x_hi: 2, x_lo: 2; x = x_hi * 2 + x_lo), y: 4, z: 16, core: 2. Of those that a mesh axis runs over, the one named last changes fastest.
Arguments:
- green_ret: bfloat16 [8, 256, 8, 2, 128, 128], P('mom', 'shard'), may hold values from -4 to 4
- broadening: bfloat16 [2, 128, 128], replicated, may hold values from -0.5 to 0.5
- occupation: float32 [8, 256], P('mom', 'shard'), may hold values from 0.1 to 1
- neighbours: int32 [64, 4], replicated, may hold values from 0 to 63, as said below
- orbitals: int32 [64], replicated, may hold values from 4 to 16
- coupling: bfloat16 [64, 4, 256, 256], P('shard'), may hold values from -0.1875 to 0.1875
- phonon: float32 [8, 2, 256], replicated, may hold values from -5 to 5
- mode_table: int32 [8, 8], replicated, may hold values from 0 to 7, as said below
Outputs:
- self_energy: bfloat16 [8, 256, 64, 2, 256], P('mom', None, 'shard')
Inputs may be any that keep to these rules, and one draw needn't show every extreme that they name: `neighbours`: row a holds 4 distinct atoms of a's own layer block (atoms 8 * (a // 8) onward), none equal to a; the first is a with its lowest bit flipped. `mode_table`: each entry names one of the 8 phonon modes.
All inputs are finite; a program needn't handle non-finite values.
Results may differ from a plain program's by a relative error of at most 0.013.
Values may be sent and summed in bfloat16 or wider, within the bound.
No kernel may reach another device: no remote copies, remote signals or barrier semaphores. Data moves between devices by JAX's collectives and lax.ppermute only.
A program may use at most 192 MiB of HBM per device.

v0:
```python
import math
import jax
import jax.numpy as jnp
from jax import lax
from jax.sharding import PartitionSpec as P

NORB = 16
ATL = 8
NBR = 4
ENERGIES = 256
LAYERS = 8
PAIR = 256
ATOMS = 64


def dft_tables(length):
    counter = jnp.arange(length, dtype=jnp.int32)
    phases = counter[:, None] * counter[None, :] % length
    angles = phases.astype(jnp.float32) * (2.0 * math.pi / length)
    return (jnp.cos(angles).astype(jnp.bfloat16), jnp.sin(angles).astype(jnp.bfloat16))


def local(green_ret, broadening, occupation, neighbours, orbitals, coupling, phonon, mode_table):
    highest = lax.Precision.HIGHEST
    greens = green_ret[0]
    energy_dev = greens.shape[0]
    mixing = jnp.stack(
        [
            jnp.concatenate([broadening[0], broadening[1]], axis=1),
            jnp.concatenate([-broadening[1], broadening[0]], axis=1),
        ],
        axis=0,
    )
    left = jnp.einsum("elpik,pkq->eliq", greens, mixing, preferred_element_type=jnp.float32).astype(
        jnp.bfloat16
    )
    slot_atoms = neighbours % ATL
    selector = slot_atoms[:, :, None] == jnp.arange(ATL, dtype=jnp.int32)[None, None, :]
    layer_orbitals = jnp.repeat(orbitals.reshape(LAYERS, ATL), ATL, axis=0)
    partner_count = jnp.sum(jnp.where(selector, layer_orbitals[:, None, :], 0), axis=2)
    green_re = greens[:, :, 0]
    green_im = greens[:, :, 1]
    partner = jnp.stack(
        [
            jnp.concatenate([green_re, green_im], axis=-1),
            jnp.concatenate([-green_im, green_re], axis=-1),
        ],
        axis=2,
    )
    blocks = jnp.einsum("elik,elpjk->elpij", left, partner, preferred_element_type=jnp.float32)
    blocks = blocks.reshape(energy_dev, LAYERS, 2, ATL, NORB, ATL, NORB).transpose(
        0, 1, 3, 5, 2, 4, 6
    )
    slot_index = slot_atoms.reshape(LAYERS, ATL, NBR)
    chosen = jnp.take_along_axis(blocks, slot_index[None, :, :, :, None, None, None], axis=3)
    chosen = chosen.reshape(energy_dev, ATOMS, NBR, 2, NORB, NORB)
    counter = jnp.arange(NORB, dtype=jnp.int32)
    row_mask = counter[None, :] < orbitals[:, None]
    column_mask = counter[None, None, :] < partner_count[:, :, None]
    pair_mask = (row_mask[:, None, :, None] & column_mask[:, :, None, :]).astype(jnp.float32)
    scaled = (
        chosen * occupation[0][:, None, None, None, None, None] * pair_mask[None, :, :, None, :, :]
    )
    pair_blocks = scaled.reshape(energy_dev, ATOMS, NBR, 2, PAIR).astype(jnp.bfloat16)
    arrived = lax.all_to_all(pair_blocks, "shard", split_axis=1, concat_axis=0, tiled=True)
    atom_dev = arrived.shape[1]
    mixed_terms = jnp.einsum(
        "eanpx,anxy->eapy", arrived, coupling, preferred_element_type=jnp.float32
    )
    first_atom = lax.axis_index("shard") * atom_dev
    own_orbitals = lax.dynamic_slice_in_dim(orbitals, first_atom, atom_dev)
    pair_index = jnp.arange(PAIR, dtype=jnp.int32)
    own_mask = (
        (pair_index[None, :] // NORB < own_orbitals[:, None])
        & (pair_index[None, :] % NORB < own_orbitals[:, None])
    ).astype(jnp.float32)
    coupled = (mixed_terms * own_mask[None, :, None, :]).astype(jnp.bfloat16)
    cos_table, sin_table = dft_tables(ENERGIES)
    flat_coupled = coupled.reshape(ENERGIES, -1)
    part_cos = jnp.dot(cos_table, flat_coupled, preferred_element_type=jnp.float32).reshape(
        ENERGIES, atom_dev, 2, PAIR
    )
    part_sin = jnp.dot(sin_table, flat_coupled, preferred_element_type=jnp.float32).reshape(
        ENERGIES, atom_dev, 2, PAIR
    )
    time_data = jnp.stack(
        [part_cos[:, :, 0] + part_sin[:, :, 1], part_cos[:, :, 1] - part_sin[:, :, 0]], axis=2
    ).astype(jnp.bfloat16)
    own_momentum = lax.axis_index("mom")
    mode_count = phonon.shape[0]
    mode_ids = jnp.arange(mode_count, dtype=jnp.int32)
    own_modes = lax.dynamic_slice_in_dim(mode_table, own_momentum, 1, 0)[0]
    phonon_flat = phonon.reshape(mode_count, -1)
    received = lax.all_gather(time_data[None], "mom", axis=0, tiled=True)
    row_count = received.shape[0]
    one_hot = (own_modes[:, None] == mode_ids[None, :]).astype(jnp.float32)
    kernel = jnp.dot(one_hot, phonon_flat, precision=highest).reshape(row_count, 2, ENERGIES)
    values = received.astype(jnp.float32)
    kernel_re = kernel[:, 0][:, :, None, None]
    kernel_im = kernel[:, 1][:, :, None, None]
    add_re = jnp.sum(kernel_re * values[:, :, :, 0] - kernel_im * values[:, :, :, 1], axis=0)
    add_im = jnp.sum(kernel_re * values[:, :, :, 1] + kernel_im * values[:, :, :, 0], axis=0)
    summed = jnp.stack([add_re, add_im], axis=2)
    convolved = summed.astype(jnp.bfloat16)
    flat_conv = convolved.reshape(ENERGIES, -1)
    back_cos = jnp.dot(cos_table, flat_conv, preferred_element_type=jnp.float32).reshape(
        ENERGIES, atom_dev, 2, PAIR
    )
    back_sin = jnp.dot(sin_table, flat_conv, preferred_element_type=jnp.float32).reshape(
        ENERGIES, atom_dev, 2, PAIR
    )
    result_re = (back_cos[:, :, 0] - back_sin[:, :, 1]) * (1.0 / ENERGIES)
    result_im = (back_cos[:, :, 1] + back_sin[:, :, 0]) * (1.0 / ENERGIES)
    return jnp.stack([result_re, result_im], axis=2)[None].astype(jnp.bfloat16)


def solution(mesh):
    in_specs = (
        P("mom", "shard", None, None, None, None),
        P(),
        P("mom", "shard"),
        P(),
        P(),
        P("shard", None, None, None),
        P(),
        P(),
    )
    out_specs = P("mom", None, "shard", None, None)
    return jax.shard_map(local, mesh=mesh, in_specs=in_specs, out_specs=out_specs, check_vma=False)
```

profile of v0, /device:TPU:1, one launch (start us, length us, event | category | flops | bytes accessed | tf_op | source)
XLA Modules:
  0.0 248.5 jit_solution(2611192785870008069)
XLA Ops:
  6.5 0.0 copy-start
  6.5 1.8 copy.111
  8.3 0.0 copy-start.2
  8.3 1.1 slice_bitcast_fusion.2
  9.4 0.0 copy-start.1
  9.4 0.1 fusion.75
  9.6 0.0 copy-done.2
  9.6 0.1 reshape.372
  9.7 0.6 copy-done.1
  10.3 0.1 copy.96
  10.4 0.1 copy.95
  10.5 4.1 %maximum_bitcast_fusion = (bf16[4,8,1,128,256]{4,3,2,1,0:T(8,128)(2,1)}, bf16[4,8,1,128,256]{4,3,2,1,0:T(8,128)(2,1)}) fusion(bf16[4,8,128,128]{3,2,1,0:T(8,128)(2,1)S(1)} %get-tuple-element.9, bf16[4,8,128,128]{3,2,1,0:T(8,128)(2,1)} %get-tuple-element.10, bf16[4,8,128,128]{3,2,1,0:T(8,128)(2,1)S(1)} %fusion.75), kind=kLoop, calls=%fused_computation.9 | loop fusion | flops 8388608 | bytes 7340032 | tf_op jit(solution)/shard_map/stack | solution.py:43
  14.7 6.8 %fusion.4 = f32[4,8,2,128,128]{3,4,2,1,0:T(8,128)} fusion(bf16[4,8,1,128,256]{4,3,2,1,0:T(8,128)(2,1)} %get-tuple-element.16, bf16[4,8,1,128,256]{4,3,2,1,0:T(8,128)(2,1)} %get-tuple-element.15, bf16[1,4,8,2,128,128]{5,4,3,2,1,0:T(8,128)(2,1)} %param.8, bf16[1,128,256]{1,2,0:T(8,128)(2,1)S(1)} %get-tuple-element.20, ...), kind=kOutput, calls=%fused_computation.6 | convolution fusion | flops 1077149696 | bytes 10616832 | tf_op jit(solution)/shard_map/elik,elpjk->elpij/dot_general | solution.py:50
  21.5 19.6 %reshape.371 = f32[4,8,2,8,16,8,16]{4,3,6,5,2,1,0:T(8,128)} reshape(f32[4,8,2,128,128]{3,4,2,1,0:T(8,128)} %fusion.4) | data formatting | bytes 8388608 | tf_op jit(solution)/shard_map/reshape | solution.py:51
  41.1 0.0 copy-start.3
  41.1 33.9 %copy.72 = f32[4,8,2,8,16,8,16]{6,4,2,5,3,1,0:T(8,128)} copy(f32[4,8,2,8,16,8,16]{4,3,6,5,2,1,0:T(8,128)} %reshape.371) | data formatting | bytes 8388608 | tf_op jit(solution)/shard_map/reshape | solution.py:51
  74.9 0.0 copy-done.3
  74.9 0.1 copy.94
  75.0 0.1 reshape.378
  75.1 14.9 %gather_fusion = f32[256,4,2,16,16]{4,3,2,1,0:T(8,128)} fusion(f32[4,8,8,8,2,16,16]{6,5,4,3,2,1,0:T(8,128)} %bitcast.180, s32[256]{0:T(256)S(1)} %reshape.378), kind=kCustom, calls=%fused_computation | custom fusion | bytes 4197376 | tf_op jit(solution)/shard_map/jit(take_along_axis)/gather | solution.py:55
  90.1 0.0 copy-start.4
  90.1 12.3 %reshape.392 = f32[4,64,4,2,256]{4,3,0,2,1:T(2,128)S(1)} reshape(f32[4,8,8,4,2,16,16]{6,5,4,0,3,2,1:T(8,128)} %bitcast.181) | data formatting | bytes 4194304 | tf_op jit(solution)/shard_map/jit(take_along_axis)/gather | solution.py:55
  102.4 0.1 copy.77
  102.5 0.1 broadcast_in_dim.26
  102.6 0.1 broadcast_in_dim.27
  102.8 0.2 copy.78
  103.0 0.1 copy.65
  103.1 0.0 copy-done.4
  103.1 1.6 fusion.10
  104.7 19.6 %all-to-all-start = ((bf16[4,64,4,2,256]{4,0,2,3,1:T(4,128)(2,1)}), bf16[4,64,4,2,256]{4,0,2,3,1:T(4,128)(2,1)S(1)}, u32[]{:S(2)}, u32[]{:S(2)}) async-start(bf16[4,64,4,2,256]{4,0,2,3,1:T(4,128)(2,1)} %fusion.10), calls=%async_computation | async-start | bytes 2097152 | tf_op jit(solution)/shard_map/all_to_all | solution.py:65
  124.3 0.0 all-gather.2.cloned.1.call-start
  124.4 0.6 dynamic_slice.7
  125.0 0.6 and_convert_fusion
  125.6 50.5 %all-to-all-done = bf16[4,64,4,2,256]{4,0,2,3,1:T(4,128)(2,1)S(1)} async-done(((bf16[4,64,4,2,256]{4,0,2,3,1:T(4,128)(2,1)}), bf16[4,64,4,2,256]{4,0,2,3,1:T(4,128)(2,1)S(1)}, u32[]{:S(2)}, u32[]{:S(2)}) %all-to-all-start) | async-done | bytes 1048608 | tf_op jit(solution)/shard_map/all_to_all | solution.py:65
  176.1 0.4 copy.79
  176.5 0.5 reshape.373
  177.0 0.0 copy-done
  177.0 0.5 fusion.18
  177.5 0.0 copy-start.5
  177.5 1.1 convolution_bitcast_fusion.2
  178.6 1.1 convolution_bitcast_fusion.3
  179.7 0.1 fusion.37
  179.8 0.7 pad_maximum_fusion
  180.6 0.0 all-gather.2.cloned.1.call-update
  180.6 0.7 dynamic-slice_bitcast_fusion
  181.3 0.0 copy-done.5
  181.3 0.2 fusion.51
  181.5 53.8 %all-gather.2.cloned.1.call-done = bf16[8,256,1,2,256]{4,1,3,2,0:T(8,128)(2,1)} async-done(((bf16[1,256,1,2,256]{4,1,3,2,0:T(8,128)(2,1)}), bf16[8,256,1,2,256]{4,1,3,2,0:T(8,128)(2,1)}) %all-gather.2.cloned.1.call-update) | async-done | bytes 2097168 | tf_op jit(solution)/shard_map/all_gather | solution.py:94
  235.3 2.0 convert_element_type.93
  237.3 0.8 subtract_reduce_fusion
  238.1 0.1 copy.82
  238.3 1.1 convolution_bitcast_fusion
  239.4 1.1 convolution_bitcast_fusion.1
  240.5 0.1 fusion.27
  240.6 1.0 copy.83
  (13 shorter events, 0.2 us)
Async XLA Ops:
  6.5 170.4 %copy-start = (bf16[1,4,256,256]{3,2,1,0:T(8,128)(2,1)S(1)}, bf16[1,4,256,256]{3,2,1,0:T(8,128)(2,1)}, u32[]{:S(2)}) copy-start(bf16[1,4,256,256]{3,2,1,0:T(8,128)(2,1)} %param.13) | copy-start | bytes 1572868
  8.3 1.3 copy-start.2
  9.4 0.8 copy-start.1
  41.1 33.9 %copy-start.3 = (s32[64,4]{0,1:T(4,128)S(1)}, s32[64,4]{0,1:T(4,128)}, u32[]{:S(2)}) copy-start(s32[64,4]{0,1:T(4,128)} %param.11) | copy-start | bytes 3076
  90.1 13.0 %copy-start.4 = (f32[1,4]{1,0:T(1,128)S(1)}, f32[1,4]{1,0:T(1,128)}, u32[]{:S(2)}) copy-start(f32[1,4]{1,0:T(1,128)} %param.10) | copy-start | bytes 52
  104.7 71.4 %all-to-all-start = ((bf16[4,64,4,2,256]{4,0,2,3,1:T(4,128)(2,1)}), bf16[4,64,4,2,256]{4,0,2,3,1:T(4,128)(2,1)S(1)}, u32[]{:S(2)}, u32[]{:S(2)}) async-start(bf16[4,64,4,2,256]{4,0,2,3,1:T(4,128)(2,1)} %fusion.10), calls=%async_computation | async-start | bytes 2097152 | tf_op jit(solution)/shard_map/all_to_all | solution.py:65
  124.3 110.9 %all-gather.2.cloned.1.call-start = ((), (), s32[]{:S(2)}) async-start(), calls=%async_computation.1 | async-start | bytes 2359296 | tf_op jit(solution)/shard_map/all_gather | solution.py:94
  177.5 3.8 %copy-start.5 = (f32[8,2,256]{2,1,0:T(2,128)S(1)}, f32[8,2,256]{2,1,0:T(2,128)}, u32[]{:S(2)}) copy-start(f32[8,2,256]{2,1,0:T(2,128)} %param.14) | copy-start | bytes 49156
Sparse Core Ops, SparseCore 0:
  180.7 54.5 all-gather.1
where the time goes:
time: 250 us; the launch traced here: 248 us
  waiting for transfers between devices  104 us (42%)
  local copies, waits for them, and re-layouts  88.6 us (35%)
  starting transfers between devices  19.6 us (8%)
  between operations  13.6 us (5%)
  matrix products  11.9 us (5%)
  other arithmetic  10.5 us (4%)
    all_gather x1, waiting for transfers between devices, local(): received = lax.all_gather(time_data[None], 'mom', axis=0, tiled=True)  53.8 us
    reshape x2, local copies, waits for them, and re-layouts, local(): blocks.reshape(energy_dev, LAYERS, 2, ATL, NORB, ATL, NORB)  53.4 us
    all_to_all x1, waiting for transfers between devices, local(): lax.all_to_all(pair_blocks, 'shard', split_axis=1, concat_axis=0, tiled=T...  50.5 us
    gather x3, local copies, waits for them, and re-layouts, local(): jnp.take_along_axis(blocks, slot_index[None, :, :, :, None, None, None],...  27.4 us
    all_to_all x1, starting transfers between devices, local(): lax.all_to_all(pair_blocks, 'shard', split_axis=1, concat_axis=0, tiled=T...  19.6 us
    dot_general x1, matrix products, local(): jnp.einsum('elik,elpjk->elpij', left, partner, preferred_element_type=jnp...  6.77 us
  transfers between devices with their start and end apart: 2, of which 2 were waited for; matrix products, arithmetic and copies ran while one was open for 1% of the time, Pallas kernels for 0%

commit v1 on v0

--- a/solution.py
+++ b/solution.py
@@ -91,7 +91,9 @@
     mode_ids = jnp.arange(mode_count, dtype=jnp.int32)
     own_modes = lax.dynamic_slice_in_dim(mode_table, own_momentum, 1, 0)[0]
     phonon_flat = phonon.reshape(mode_count, -1)
-    received = lax.all_gather(time_data[None], "mom", axis=0, tiled=True)
+    received = jnp.concatenate(
+        lax.all_to_all(jnp.stack([time_data[None]] * lax.axis_size("mom")), "mom", 0, 0), axis=0
+    )
     row_count = received.shape[0]
     one_hot = (own_modes[:, None] == mode_ids[None, :]).astype(jnp.float32)
     kernel = jnp.dot(one_hot, phonon_flat, precision=highest).reshape(row_count, 2, ENERGIES)

time: 250 us -> 214 us (0.86); the launches traced: 248 us -> 210 us
  waiting for transfers between devices: 104 us -> 75.6 us
  between operations: 13.6 us -> 0.22 us
  starting transfers between devices: 19.6 us -> 24.1 us
    all_gather x1 -> x0, waiting for transfers between devices: 53.8 us -> none  [local(): received = lax.all_gather(time_data[None], 'mom', axis=0, tiled=True)]
    all_to_all x0 -> x1, waiting for transfers between devices: none -> 25 us  [local(): lax.all_to_all(jnp.stack([time_data[None]] * lax.axis_size('mom')), 'mom'...]
    all_to_all x0 -> x1, starting transfers between devices: none -> 4.36 us  [local(): lax.all_to_all(jnp.stack([time_data[None]] * lax.axis_size('mom')), 'mom'...]
where the time goes in v1:
time: 214 us; the launch traced here: 210 us
  local copies, waits for them, and re-layouts  89.9 us (42%)
  waiting for transfers between devices  75.6 us (35%)
  starting transfers between devices  24.1 us (11%)
  matrix products  11.9 us (6%)
  other arithmetic  8.15 us (4%)
    reshape x2, local copies, waits for them, and re-layouts, local(): blocks.reshape(energy_dev, LAYERS, 2, ATL, NORB, ATL, NORB)  53.4 us
    all_to_all x1, waiting for transfers between devices, local(): lax.all_to_all(pair_blocks, 'shard', split_axis=1, concat_axis=0, tiled=T...  50.5 us
    gather x3, local copies, waits for them, and re-layouts, local(): jnp.take_along_axis(blocks, slot_index[None, :, :, :, None, None, None],...  27.4 us
    all_to_all x1, waiting for transfers between devices, local(): lax.all_to_all(jnp.stack([time_data[None]] * lax.axis_size('mom')), 'mom'...  25 us
    all_to_all x1, starting transfers between devices, local(): lax.all_to_all(pair_blocks, 'shard', split_axis=1, concat_axis=0, tiled=T...  19.8 us
    dot_general x1, matrix products, local(): jnp.einsum('elik,elpjk->elpij', left, partner, preferred_element_type=jnp...  6.77 us
    all_to_all x1, starting transfers between devices, local(): lax.all_to_all(jnp.stack([time_data[None]] * lax.axis_size('mom')), 'mom'...  4.36 us
  transfers between devices with their start and end apart: 2, of which 2 were waited for; matrix products, arithmetic and copies ran while one was open for 1% of the time, Pallas kernels for 0%

profile of v1, /device:TPU:1, one launch (start us, length us, event | category | flops | bytes accessed | tf_op | source)
XLA Modules:
  0.0 209.8 jit_solution(11283144335257559622)
XLA Ops:
  0.0 0.0 copy-start
  0.0 1.8 copy.129
  1.8 0.0 copy-start.2
  1.8 1.1 slice_bitcast_fusion.2
  2.9 0.0 copy-start.1
  2.9 0.1 fusion.75
  3.0 0.0 copy-done.2
  3.1 0.1 reshape.379
  3.1 0.6 copy-done.1
  3.7 0.1 copy.114
  3.9 0.1 copy.113
  4.0 4.1 %maximum_bitcast_fusion = (bf16[4,8,1,128,256]{4,3,2,1,0:T(8,128)(2,1)}, bf16[4,8,1,128,256]{4,3,2,1,0:T(8,128)(2,1)}) fusion(bf16[4,8,128,128]{3,2,1,0:T(8,128)(2,1)S(1)} %get-tuple-element.9, bf16[4,8,128,128]{3,2,1,0:T(8,128)(2,1)} %get-tuple-element.10, bf16[4,8,128,128]{3,2,1,0:T(8,128)(2,1)S(1)} %fusion.75), kind=kLoop, calls=%fused_computation.9 | loop fusion | flops 8388608 | bytes 7340032 | tf_op jit(solution)/shard_map/stack | solution.py:43
  8.1 6.8 %fusion.4 = f32[4,8,2,128,128]{3,4,2,1,0:T(8,128)} fusion(bf16[4,8,1,128,256]{4,3,2,1,0:T(8,128)(2,1)} %get-tuple-element.16, bf16[4,8,1,128,256]{4,3,2,1,0:T(8,128)(2,1)} %get-tuple-element.15, bf16[1,4,8,2,128,128]{5,4,3,2,1,0:T(8,128)(2,1)} %param.8, bf16[1,128,256]{1,2,0:T(8,128)(2,1)S(1)} %get-tuple-element.20, ...), kind=kOutput, calls=%fused_computation.6 | convolution fusion | flops 1077149696 | bytes 10616832 | tf_op jit(solution)/shard_map/elik,elpjk->elpij/dot_general | solution.py:50
  14.9 19.6 %reshape.378 = f32[4,8,2,8,16,8,16]{4,3,6,5,2,1,0:T(8,128)} reshape(f32[4,8,2,128,128]{3,4,2,1,0:T(8,128)} %fusion.4) | data formatting | bytes 8388608 | tf_op jit(solution)/shard_map/reshape | solution.py:51
  34.5 0.0 copy-start.3
  34.5 33.9 %copy.88 = f32[4,8,2,8,16,8,16]{6,4,2,5,3,1,0:T(8,128)} copy(f32[4,8,2,8,16,8,16]{4,3,6,5,2,1,0:T(8,128)} %reshape.378) | data formatting | bytes 8388608 | tf_op jit(solution)/shard_map/reshape | solution.py:51
  68.4 0.0 copy-done.3
  68.4 0.1 copy.112
  68.5 0.1 reshape.386
  68.6 14.9 %gather_fusion = f32[256,4,2,16,16]{4,3,2,1,0:T(8,128)} fusion(f32[4,8,8,8,2,16,16]{6,5,4,3,2,1,0:T(8,128)} %bitcast.187, s32[256]{0:T(256)S(1)} %reshape.386), kind=kCustom, calls=%fused_computation | custom fusion | bytes 4197376 | tf_op jit(solution)/shard_map/jit(take_along_axis)/gather | solution.py:55
  83.5 0.0 copy-start.4
  83.5 12.3 %reshape.400 = f32[4,64,4,2,256]{4,3,0,2,1:T(2,128)S(1)} reshape(f32[4,8,8,4,2,16,16]{6,5,4,0,3,2,1:T(8,128)} %bitcast.188) | data formatting | bytes 4194304 | tf_op jit(solution)/shard_map/jit(take_along_axis)/gather | solution.py:55
  95.9 0.1 copy.93
  96.0 0.1 broadcast_in_dim.26
  96.0 0.1 broadcast_in_dim.27
  96.2 0.2 copy.94
  96.4 0.1 copy.81
  96.5 0.0 copy-done.4
  96.5 1.6 fusion.10
  98.2 19.8 %all-to-all-start = ((bf16[4,64,4,2,256]{4,0,2,3,1:T(4,128)(2,1)}), bf16[4,64,4,2,256]{4,0,2,3,1:T(4,128)(2,1)S(1)}, u32[]{:S(2)}, u32[]{:S(2)}) async-start(bf16[4,64,4,2,256]{4,0,2,3,1:T(4,128)(2,1)} %fusion.10), calls=%async_computation | async-start | bytes 2097152 | tf_op jit(solution)/shard_map/all_to_all | solution.py:65
  118.0 0.6 dynamic_slice.7
  118.5 0.6 and_convert_fusion
  119.2 50.5 %all-to-all-done = bf16[4,64,4,2,256]{4,0,2,3,1:T(4,128)(2,1)S(1)} async-done(((bf16[4,64,4,2,256]{4,0,2,3,1:T(4,128)(2,1)}), bf16[4,64,4,2,256]{4,0,2,3,1:T(4,128)(2,1)S(1)}, u32[]{:S(2)}, u32[]{:S(2)}) %all-to-all-start) | async-done | bytes 1048608 | tf_op jit(solution)/shard_map/all_to_all | solution.py:65
  169.7 0.4 copy.95
  170.1 0.3 reshape.380
  170.4 0.0 copy-done
  170.4 0.5 fusion.18
  170.9 1.1 convolution_bitcast_fusion.2
  172.0 1.1 convolution_bitcast_fusion.3
  173.1 0.1 fusion.37
  173.3 1.5 stack.54
  174.8 0.0 copy-start.5
  174.8 4.4 %all-to-all-start.1 = ((bf16[8,1,256,1,2,256]{5,2,4,3,1,0:T(8,128)(2,1)}), bf16[8,1,256,1,2,256]{5,2,4,3,1,0:T(8,128)(2,1)S(1)}, u32[]{:S(2)}, u32[]{:S(2)}) async-start(bf16[8,1,256,1,2,256]{5,2,4,3,1,0:T(8,128)(2,1)} %stack.54), calls=%async_computation.1 | async-start | bytes 4194304 | tf_op jit(solution)/shard_map/all_to_all | solution.py:95
  179.2 0.7 dynamic-slice_bitcast_fusion
  179.9 0.0 copy-done.5
  179.9 0.2 fusion.51
  180.1 25.0 %all-to-all-done.1 = bf16[8,1,256,1,2,256]{5,2,4,3,1,0:T(8,128)(2,1)S(1)} async-done(((bf16[8,1,256,1,2,256]{5,2,4,3,1,0:T(8,128)(2,1)}), bf16[8,1,256,1,2,256]{5,2,4,3,1,0:T(8,128)(2,1)S(1)}, u32[]{:S(2)}, u32[]{:S(2)}) %all-to-all-start.1) | async-done | bytes 2097184 | tf_op jit(solution)/shard_map/all_to_all | solution.py:95
  205.1 0.4 bitcast_convert_fusion.1
  205.5 0.8 bitcast_reduce_fusion.1
  206.4 0.1 copy.100
  206.5 1.1 convolution_bitcast_fusion
  207.6 1.1 convolution_bitcast_fusion.1
  208.8 0.1 fusion.27
  208.9 1.0 copy.101
  (14 shorter events, 0.2 us)
Async XLA Ops:
  0.0 170.4 %copy-start = (bf16[1,4,256,256]{3,2,1,0:T(8,128)(2,1)S(1)}, bf16[1,4,256,256]{3,2,1,0:T(8,128)(2,1)}, u32[]{:S(2)}) copy-start(bf16[1,4,256,256]{3,2,1,0:T(8,128)(2,1)} %param.13) | copy-start | bytes 1572868
  1.8 1.3 copy-start.2
  2.9 0.8 copy-start.1
  34.5 33.9 %copy-start.3 = (s32[64,4]{0,1:T(4,128)S(1)}, s32[64,4]{0,1:T(4,128)}, u32[]{:S(2)}) copy-start(s32[64,4]{0,1:T(4,128)} %param.11) | copy-start | bytes 3076
  83.5 13.0 %copy-start.4 = (f32[1,4]{1,0:T(1,128)S(1)}, f32[1,4]{1,0:T(1,128)}, u32[]{:S(2)}) copy-start(f32[1,4]{1,0:T(1,128)} %param.10) | copy-start | bytes 52
  98.2 71.6 %all-to-all-start = ((bf16[4,64,4,2,256]{4,0,2,3,1:T(4,128)(2,1)}), bf16[4,64,4,2,256]{4,0,2,3,1:T(4,128)(2,1)S(1)}, u32[]{:S(2)}, u32[]{:S(2)}) async-start(bf16[4,64,4,2,256]{4,0,2,3,1:T(4,128)(2,1)} %fusion.10), calls=%async_computation | async-start | bytes 2097152 | tf_op jit(solution)/shard_map/all_to_all | solution.py:65
  174.8 5.1 %copy-start.5 = (f32[8,2,256]{2,1,0:T(2,128)S(1)}, f32[8,2,256]{2,1,0:T(2,128)}, u32[]{:S(2)}) copy-start(f32[8,2,256]{2,1,0:T(2,128)} %param.14) | copy-start | bytes 49156
  174.8 30.3 %all-to-all-start.1 = ((bf16[8,1,256,1,2,256]{5,2,4,3,1,0:T(8,128)(2,1)}), bf16[8,1,256,1,2,256]{5,2,4,3,1,0:T(8,128)(2,1)S(1)}, u32[]{:S(2)}, u32[]{:S(2)}) async-start(bf16[8,1,256,1,2,256]{5,2,4,3,1,0:T(8,128)(2,1)} %stack.54), calls=%async_computation.1 | async-start | bytes 4194304 | tf_op jit(solution)/shard_map/all_to_all | solution.py:95
